TPU v7x, 32 devices: a whole 2x2x4 slice. The times are simulated.
32 devices in a mesh: seq: 8 (over z, x), head: 4 (over y, core).
Axes of the slice: x: 2, y: 2, z: 4, core: 2. Of those that a mesh axis runs over, the one named last changes fastest.
Arguments:
- queries: bfloat16 [2048, 4096], P('seq', 'head'), may hold values from -100 to 100
- keys_values: bfloat16 [2048, 2, 512], P('seq', None, 'head'), may hold values from -4.5 to 4.5
- cache_kv: bfloat16 [2048, 2, 512], P('seq', None, 'head'), may hold values from -4 to 4
- vertical_pages: int32 [4, 4], P('head'), may hold values from 0 to 15, as said below
- slash_shift: int32 [4, 3], P('head'), may hold values from 1 to 8, as said below
- slash_live: int32 [8, 4, 3], P('seq', 'head'), may hold values 0 or 1
- out_proj: bfloat16 [4096, 2048], P('head'), may hold values from -0.09375 to 0.09375
Outputs:
- projected: bfloat16 [2048, 2048], P('seq', 'head')
Inputs may be any that keep to these rules, and one draw needn't show every extreme that they name: `vertical_pages`: each head group lists 4 distinct pages. `slash_shift`: each head group lists 3 distinct distances.
All inputs are finite; a program needn't handle non-finite values. No bound on the sum of `slash_live` on one device may be relied on, other than what follows from the above.
Results may differ from a plain program's by a relative error of at most 0.0057.
Values may be sent and summed in bfloat16 or wider, within the bound.
No kernel may reach another device: no remote copies, remote signals or barrier semaphores. Data moves between devices by JAX's collectives and lax.ppermute only.
A program may use at most 64 MiB of HBM per device.

v0:
```python
import jax
import jax.numpy as jnp
from jax import lax
from jax.sharding import PartitionSpec as P

PAGE = 128


def passed_along(value, axis, steps):
    count = lax.axis_size(axis)
    pairs = [(source, (source + steps) % count) for source in range(count)]
    return lax.ppermute(value, axis, pairs)


def rotate(stacked, amounts, shards):
    reduced = amounts % shards
    for bit_number in range(max(1, (shards - 1).bit_length())):
        moved = passed_along(stacked, "seq", 1 << bit_number)
        chosen = reduced // (1 << bit_number) % 2 == 1
        stacked = jnp.where(chosen[:, None, None, None], moved, stacked)
    return stacked


def body(queries, keys_values, cache_kv, vertical_pages, slash_shift, slash_live, out_proj):
    row_count = queries.shape[0]
    head_width = keys_values.shape[2]
    group_heads = queries.shape[1] // head_width
    shards = lax.axis_size("seq")
    own_shard = lax.axis_index("seq")
    distances = slash_shift[0]
    live_blocks = slash_live[0, 0] == 1
    page_ids = vertical_pages[0]
    slash_count = distances.shape[0]
    payload = jnp.where(
        (own_shard < shards - distances)[:, None, None, None], keys_values[None], cache_kv[None]
    )
    slash_kv = jnp.concatenate(
        [
            rotate(payload[position : position + 1], distances[position : position + 1], shards)
            for position in range(slash_count)
        ],
        0,
    )
    per_shard = row_count // PAGE
    owners = page_ids // per_shard
    whole_cache = lax.all_gather(cache_kv, "seq", axis=0, tiled=True)
    vertical = jax.vmap(
        lambda page_key: lax.dynamic_slice_in_dim(whole_cache, page_key * PAGE, PAGE, 0)
    )(page_ids)
    cached_slash = own_shard + shards - distances
    clash = (
        live_blocks[None, :]
        & (distances[None, :] > own_shard)
        & (owners[:, None] == cached_slash[None, :])
    )
    page_open = jnp.logical_not(jnp.any(clash, axis=1))
    row_ids = lax.broadcasted_iota(jnp.int32, (row_count, row_count), 0)
    col_ids = lax.broadcasted_iota(jnp.int32, (row_count, row_count), 1)
    causal = row_ids >= col_ids
    column_open = jnp.concatenate([jnp.repeat(live_blocks, row_count), jnp.repeat(page_open, PAGE)])
    visible = jnp.concatenate(
        [causal, jnp.broadcast_to(column_open[None, :], (row_count, column_open.shape[0]))], 1
    )
    all_keys = jnp.concatenate(
        [keys_values, slash_kv.reshape(-1, 2, head_width), vertical.reshape(-1, 2, head_width)], 0
    )
    query_heads = queries.reshape(row_count, group_heads, head_width)
    scores = jnp.einsum(
        "rgd,kd->grk", query_heads, all_keys[:, 0, :], preferred_element_type=jnp.float32
    )
    scores = scores * head_width ** (-0.5)
    scores = jnp.where(visible[None], scores, -jnp.inf)
    row_max = jnp.max(scores, axis=2, keepdims=True)
    weights = jnp.exp(scores - row_max)
    row_total = jnp.sum(weights, axis=2, keepdims=True)
    weights_bf = (weights / row_total).astype(jnp.bfloat16)
    attended = jnp.einsum(
        "grk,kd->rgd", weights_bf, all_keys[:, 1, :], preferred_element_type=jnp.float32
    )
    attended = attended.astype(jnp.bfloat16).reshape(row_count, group_heads * head_width)
    group_terms = jnp.dot(attended, out_proj, preferred_element_type=jnp.float32)
    return lax.psum_scatter(group_terms, "head", scatter_dimension=1, tiled=True).astype(
        jnp.bfloat16
    )


def solution(mesh):
    placed = (
        P("seq", "head"),
        P("seq", None, "head"),
        P("seq", None, "head"),
        P("head", None),
        P("head", None),
        P("seq", "head", None),
        P("head", None),
    )
    return jax.shard_map(
        body, mesh=mesh, in_specs=placed, out_specs=P("seq", "head"), check_vma=False
    )
```

profile of v0, /device:TPU:0, one launch (start us, length us, event | category | flops | bytes accessed | tf_op | source)
XLA Modules:
  0.0 124.2 jit_solution(2235613061482874402)
XLA Ops:
  6.5 0.0 copy-start
  6.5 0.0 all-gather.2.cloned.1.call-start
  6.5 0.7 all-gather.2.cloned.1.call-update
  7.3 0.0 reduce-scatter.2.cloned.1.call-start
  7.3 0.9 copy.23
  8.2 0.9 copy.25
  9.2 0.7 compare_bitcast_fusion
  9.8 0.1 broadcast_select_fusion
  10.0 3.0 %collective-permute-start = (bf16[1,256,2,128]{3,1,0,2:T(8,128)(2,1)S(1)}, bf16[1,256,2,128]{3,1,0,2:T(8,128)(2,1)S(1)}, u32[]{:S(2)}, u32[]{:S(2)}) collective-permute-start(bf16[1,256,2,128]{3,1,0,2:T(8,128)(2,1)S(1)} %get-tuple-element.8), channel_id=1, source_target_pairs={{0,4},{4,8},{8,12},{12,16},{16,20},{20,24},{24,28},{28,0},{1,5},{5... | collective-permute-start | bytes 393224 | tf_op jit(solution)/shard_map/ppermute | solution.py:12
  13.0 1.5 %collective-permute-start.6 = (bf16[1,256,2,128]{3,1,0,2:T(8,128)(2,1)S(1)}, bf16[1,256,2,128]{3,1,0,2:T(8,128)(2,1)S(1)}, u32[]{:S(2)}, u32[]{:S(2)}) collective-permute-start(bf16[1,256,2,128]{3,1,0,2:T(8,128)(2,1)S(1)} %get-tuple-element.9), channel_id=1, source_target_pairs={{0,4},{4,8},{8,12},{12,16},{16,20},{20,24},{24,28},{28,0},{1,5},{5... | collective-permute-start | bytes 393224 | tf_op jit(solution)/shard_map/ppermute | solution.py:12
  14.6 1.5 %collective-permute-start.3 = (bf16[1,256,2,128]{3,1,0,2:T(8,128)(2,1)S(1)}, bf16[1,256,2,128]{3,1,0,2:T(8,128)(2,1)S(1)}, u32[]{:S(2)}, u32[]{:S(2)}) collective-permute-start(bf16[1,256,2,128]{3,1,0,2:T(8,128)(2,1)S(1)} %get-tuple-element.10), channel_id=1, source_target_pairs={{0,4},{4,8},{8,12},{12,16},{16,20},{20,24},{24,28},{28,0},{1,5},{5... | collective-permute-start | bytes 393224 | tf_op jit(solution)/shard_map/ppermute | solution.py:12
  16.1 0.7 compare_bitcast_fusion.1
  16.7 0.7 subtract_bitcast_fusion
  17.4 0.7 and_select_fusion
  18.1 0.1 broadcast_in_dim.154
  18.2 0.2 and_reduce_fusion
  18.4 0.1 broadcast_bitcast_fusion
  18.5 0.3 pad_add_fusion
  18.7 1.4 %fusion.27 = (s32[1,1]{1,0:T(1,128)}, s32[1,1]{1,0:T(1,128)}, s32[1,1]{1,0:T(1,128)}) fusion(s32[1,3]{1,0:T(1,128)} %param.11), kind=kLoop, calls=%fused_computation.53 | loop fusion | bytes 24 | tf_op jit(solution)/shard_map/slice | solution.py:39
  25.9 0.0 collective-permute-done
  25.9 0.0 collective-permute-done.6
  25.9 0.0 collective-permute-done.3
  26.0 1.6 %collective-permute-start.1 = (bf16[1,256,2,128]{3,1,0,2:T(8,128)(2,1)S(1)}, bf16[1,256,2,128]{3,1,0,2:T(8,128)(2,1)S(1)}, u32[]{:S(2)}, u32[]{:S(2)}) collective-permute-start(bf16[1,256,2,128]{3,1,0,2:T(8,128)(2,1)S(1)} %get-tuple-element.5), channel_id=1, source_target_pairs={{0,8},{4,12},{8,16},{12,20},{16,24},{20,28},{24,0},{28,4},{1,9},{5... | collective-permute-start | bytes 393224 | tf_op jit(solution)/shard_map/ppermute | solution.py:12
  27.6 0.7 fusion.23
  28.3 1.6 %collective-permute-start.4 = (bf16[1,256,2,128]{3,1,0,2:T(8,128)(2,1)S(1)}, bf16[1,256,2,128]{3,1,0,2:T(8,128)(2,1)S(1)}, u32[]{:S(2)}, u32[]{:S(2)}) collective-permute-start(bf16[1,256,2,128]{3,1,0,2:T(8,128)(2,1)S(1)} %get-tuple-element.6), channel_id=1, source_target_pairs={{0,8},{4,12},{8,16},{12,20},{16,24},{20,28},{24,0},{28,4},{1,9},{5... | collective-permute-start | bytes 393224 | tf_op jit(solution)/shard_map/ppermute | solution.py:12
  29.9 0.3 collective-permute-start.7
  30.2 4.6 %collective-permute-done.1 = bf16[1,256,2,128]{3,1,0,2:T(8,128)(2,1)S(1)} collective-permute-done((bf16[1,256,2,128]{3,1,0,2:T(8,128)(2,1)S(1)}, bf16[1,256,2,128]{3,1,0,2:T(8,128)(2,1)S(1)}, u32[]{:S(2)}, u32[]{:S(2)}) %collective-permute-start.1) | collective-permute-done | bytes 131104 | tf_op jit(solution)/shard_map/ppermute | solution.py:12
  34.8 1.5 %collective-permute-start.2 = (bf16[1,256,2,128]{3,1,0,2:T(8,128)(2,1)S(1)}, bf16[1,256,2,128]{3,1,0,2:T(8,128)(2,1)S(1)}, u32[]{:S(2)}, u32[]{:S(2)}) collective-permute-start(bf16[1,256,2,128]{3,1,0,2:T(8,128)(2,1)S(1)} %broadcast_select_fusion.8), channel_id=1, source_target_pairs={{0,16},{4,20},{8,24},{12,28},{16,0},{20,4},{24,8},{28,12},{1,17},{... | collective-permute-start | bytes 393224 | tf_op jit(solution)/shard_map/ppermute | solution.py:12
  36.3 1.3 %collective-permute-done.4 = bf16[1,256,2,128]{3,1,0,2:T(8,128)(2,1)S(1)} collective-permute-done((bf16[1,256,2,128]{3,1,0,2:T(8,128)(2,1)S(1)}, bf16[1,256,2,128]{3,1,0,2:T(8,128)(2,1)S(1)}, u32[]{:S(2)}, u32[]{:S(2)}) %collective-permute-start.4) | collective-permute-done | bytes 131104 | tf_op jit(solution)/shard_map/ppermute | solution.py:12
  37.6 1.5 %collective-permute-start.5 = (bf16[1,256,2,128]{3,1,0,2:T(8,128)(2,1)S(1)}, bf16[1,256,2,128]{3,1,0,2:T(8,128)(2,1)S(1)}, u32[]{:S(2)}, u32[]{:S(2)}) collective-permute-start(bf16[1,256,2,128]{3,1,0,2:T(8,128)(2,1)S(1)} %broadcast_select_fusion.5), channel_id=1, source_target_pairs={{0,16},{4,20},{8,24},{12,28},{16,0},{20,4},{24,8},{28,12},{1,17},{... | collective-permute-start | bytes 393224 | tf_op jit(solution)/shard_map/ppermute | solution.py:12
  39.1 1.3 %collective-permute-done.7 = bf16[1,256,2,128]{3,1,0,2:T(8,128)(2,1)S(1)} collective-permute-done((bf16[1,256,2,128]{3,1,0,2:T(8,128)(2,1)S(1)}, bf16[1,256,2,128]{3,1,0,2:T(8,128)(2,1)S(1)}, u32[]{:S(2)}, u32[]{:S(2)}) %collective-permute-start.7) | collective-permute-done | bytes 131104 | tf_op jit(solution)/shard_map/ppermute | solution.py:12
  40.4 8.5 %collective-permute-start.8 = (bf16[1,256,2,128]{3,1,0,2:T(8,128)(2,1)S(1)}, bf16[1,256,2,128]{3,1,0,2:T(8,128)(2,1)S(1)}, u32[]{:S(2)}, u32[]{:S(2)}) collective-permute-start(bf16[1,256,2,128]{3,1,0,2:T(8,128)(2,1)S(1)} %broadcast_select_fusion.2), channel_id=1, source_target_pairs={{0,16},{4,20},{8,24},{12,28},{16,0},{20,4},{24,8},{28,12},{1,17},{... | collective-permute-start | bytes 393224 | tf_op jit(solution)/shard_map/ppermute | solution.py:12
  49.0 0.7 collective-permute-done.2
  49.7 4.2 %collective-permute-done.5 = bf16[1,256,2,128]{3,1,0,2:T(8,128)(2,1)S(1)} collective-permute-done((bf16[1,256,2,128]{3,1,0,2:T(8,128)(2,1)S(1)}, bf16[1,256,2,128]{3,1,0,2:T(8,128)(2,1)S(1)}, u32[]{:S(2)}, u32[]{:S(2)}) %collective-permute-start.5) | collective-permute-done | bytes 131104 | tf_op jit(solution)/shard_map/ppermute | solution.py:12
  53.9 6.4 %collective-permute-done.8 = bf16[1,256,2,128]{3,1,0,2:T(8,128)(2,1)S(1)} collective-permute-done((bf16[1,256,2,128]{3,1,0,2:T(8,128)(2,1)S(1)}, bf16[1,256,2,128]{3,1,0,2:T(8,128)(2,1)S(1)}, u32[]{:S(2)}, u32[]{:S(2)}) %collective-permute-start.8) | collective-permute-done | bytes 131104 | tf_op jit(solution)/shard_map/ppermute | solution.py:12
  60.4 7.5 %all-gather.2.cloned.1.call-done = bf16[2048,2,128]{2,1,0:T(2,128)(2,1)} async-done(((bf16[256,2,128]{2,1,0:T(2,128)(2,1)}), bf16[2048,2,128]{2,1,0:T(2,128)(2,1)}) %all-gather.2.cloned.1.call-update) | async-done | bytes 1048592 | tf_op jit(solution)/shard_map/all_gather | solution.py:46
  67.8 2.3 %gather_fusion = bf16[4,128,2,128]{3,2,1,0:T(2,128)(2,1)S(1)} fusion(bf16[2048,2,128]{2,1,0:T(2,128)(2,1)} %all-gather.2.cloned.1.call-done, s32[4]{0:T(128)S(1)} %fusion.23), kind=kCustom, calls=%fused_computation | custom fusion | bytes 524336 | tf_op jit(solution)/shard_map/vmap()/gather | solution.py:48
  70.2 0.1 pad_maximum_fusion
  70.2 0.0 copy-done
  70.3 6.9 %fusion.28 = (f32[8,256]{1,0:T(8,128)S(1)}, f32[8,256,1536]{1,2,0:T(8,128)}) fusion(pred[256,1536]{0,1:T(8,128)(4,1)S(1)} %pad_add_fusion, bf16[1536,2,128]{2,0,1:T(8,128)(2,1)S(1)} %pad_maximum_fusion, bf16[256,1024]{1,0:T(8,128)(2,1)S(1)} %copy-done), kind=kOutput, calls=%fused_computation.54 | convolution fusion | flops 817890816 | bytes 13901824 | tf_op jit(solution)/shard_map/sub | solution.py:74
  77.2 0.0 copy-start.1
  77.2 5.7 %fusion.8 = bf16[128,8,256]{2,0,1:T(8,128)(2,1)S(1)} fusion(f32[8,256,1536]{1,2,0:T(8,128)} %get-tuple-element.17, f32[8,256]{1,0:T(8,128)S(1)} %get-tuple-element.16, bf16[1536,2,128]{2,0,1:T(8,128)(2,1)S(1)} %pad_maximum_fusion), kind=kOutput, calls=%fused_computation.12 | convolution fusion | flops 811859968 | bytes 13508608 | tf_op jit(solution)/shard_map/grk,kd->rgd/dot_general | solution.py:77
  82.9 0.0 copy-done.1
  83.0 2.6 %fusion.33 = f32[256,2048]{1,0:T(8,128)} fusion(bf16[256,1024]{0,1:T(8,128)(2,1)S(1)} %bitcast.95, bf16[1024,2048]{1,0:T(8,128)(2,1)S(1)} %copy-done.1), kind=kOutput, calls=%fused_computation.55 | convolution fusion | flops 1073741824 | bytes 6815744 | tf_op jit(solution)/shard_map/dot_general | solution.py:81
  85.6 0.0 reduce-scatter.2.cloned.1.call-update
  85.6 30.0 %reduce-scatter.2.cloned.1.call-done = f32[256,512]{1,0:T(8,128)} async-done(((f32[256,2048]{1,0:T(8,128)}), f32[256,512]{1,0:T(8,128)}) %reduce-scatter.2.cloned.1.call-update) | async-done | bytes 524304 | tf_op jit(solution)/shard_map/reduce_scatter | solution.py:82
  115.6 1.8 %convert_element_type.15 = bf16[256,512]{1,0:T(8,128)(2,1)} convert(f32[256,512]{1,0:T(8,128)} %reduce-scatter.2.cloned.1.call-done) | non-fusion elementwise | flops 131072 | bytes 786432 | tf_op jit(solution)/shard_map/convert_element_type | solution.py:82
  (15 shorter events, 0.3 us)
Async XLA Ops:
  6.5 63.7 %copy-start = (bf16[256,1024]{1,0:T(8,128)(2,1)S(1)}, bf16[256,1024]{1,0:T(8,128)(2,1)}, u32[]{:S(2)}) copy-start(bf16[256,1024]{1,0:T(8,128)(2,1)} %param.7) | copy-start | bytes 1572868
  6.5 61.3 %all-gather.2.cloned.1.call-start = ((), (), s32[]{:S(2)}) async-start(), calls=%async_computation.1 | async-start | bytes 1179648 | tf_op jit(solution)/shard_map/all_gather | solution.py:46
  7.3 108.3 %reduce-scatter.2.cloned.1.call-start = ((), (), s32[]{:S(2)}) async-start(), calls=%async_computation.2 | async-start | bytes 2621440 | tf_op jit(solution)/shard_map/reduce_scatter | solution.py:82
  10.0 15.9 %collective-permute-start = (bf16[1,256,2,128]{3,1,0,2:T(8,128)(2,1)S(1)}, bf16[1,256,2,128]{3,1,0,2:T(8,128)(2,1)S(1)}, u32[]{:S(2)}, u32[]{:S(2)}) collective-permute-start(bf16[1,256,2,128]{3,1,0,2:T(8,128)(2,1)S(1)} %get-tuple-element.8), channel_id=1, source_target_pairs={{0,4},{4,8},{8,12},{12,16},{16,20},{20,24},{24,28},{28,0},{1,5},{5... | collective-permute-start | bytes 393224 | tf_op jit(solution)/shard_map/ppermute | solution.py:12
  13.0 12.9 %collective-permute-start.6 = (bf16[1,256,2,128]{3,1,0,2:T(8,128)(2,1)S(1)}, bf16[1,256,2,128]{3,1,0,2:T(8,128)(2,1)S(1)}, u32[]{:S(2)}, u32[]{:S(2)}) collective-permute-start(bf16[1,256,2,128]{3,1,0,2:T(8,128)(2,1)S(1)} %get-tuple-element.9), channel_id=1, source_target_pairs={{0,4},{4,8},{8,12},{12,16},{16,20},{20,24},{24,28},{28,0},{1,5},{5... | collective-permute-start | bytes 393224 | tf_op jit(solution)/shard_map/ppermute | solution.py:12
  14.6 11.4 %collective-permute-start.3 = (bf16[1,256,2,128]{3,1,0,2:T(8,128)(2,1)S(1)}, bf16[1,256,2,128]{3,1,0,2:T(8,128)(2,1)S(1)}, u32[]{:S(2)}, u32[]{:S(2)}) collective-permute-start(bf16[1,256,2,128]{3,1,0,2:T(8,128)(2,1)S(1)} %get-tuple-element.10), channel_id=1, source_target_pairs={{0,4},{4,8},{8,12},{12,16},{16,20},{20,24},{24,28},{28,0},{1,5},{5... | collective-permute-start | bytes 393224 | tf_op jit(solution)/shard_map/ppermute | solution.py:12
  26.0 8.8 %collective-permute-start.1 = (bf16[1,256,2,128]{3,1,0,2:T(8,128)(2,1)S(1)}, bf16[1,256,2,128]{3,1,0,2:T(8,128)(2,1)S(1)}, u32[]{:S(2)}, u32[]{:S(2)}) collective-permute-start(bf16[1,256,2,128]{3,1,0,2:T(8,128)(2,1)S(1)} %get-tuple-element.5), channel_id=1, source_target_pairs={{0,8},{4,12},{8,16},{12,20},{16,24},{20,28},{24,0},{28,4},{1,9},{5... | collective-permute-start | bytes 393224 | tf_op jit(solution)/shard_map/ppermute | solution.py:12
  28.3 9.3 %collective-permute-start.4 = (bf16[1,256,2,128]{3,1,0,2:T(8,128)(2,1)S(1)}, bf16[1,256,2,128]{3,1,0,2:T(8,128)(2,1)S(1)}, u32[]{:S(2)}, u32[]{:S(2)}) collective-permute-start(bf16[1,256,2,128]{3,1,0,2:T(8,128)(2,1)S(1)} %get-tuple-element.6), channel_id=1, source_target_pairs={{0,8},{4,12},{8,16},{12,20},{16,24},{20,28},{24,0},{28,4},{1,9},{5... | collective-permute-start | bytes 393224 | tf_op jit(solution)/shard_map/ppermute | solution.py:12
  29.9 10.5 %collective-permute-start.7 = (bf16[1,256,2,128]{3,1,0,2:T(8,128)(2,1)S(1)}, bf16[1,256,2,128]{3,1,0,2:T(8,128)(2,1)S(1)}, u32[]{:S(2)}, u32[]{:S(2)}) collective-permute-start(bf16[1,256,2,128]{3,1,0,2:T(8,128)(2,1)S(1)} %get-tuple-element.7), channel_id=1, source_target_pairs={{0,8},{4,12},{8,16},{12,20},{16,24},{20,28},{24,0},{28,4},{1,9},{5... | collective-permute-start | bytes 393224 | tf_op jit(solution)/shard_map/ppermute | solution.py:12
  34.8 14.8 %collective-permute-start.2 = (bf16[1,256,2,128]{3,1,0,2:T(8,128)(2,1)S(1)}, bf16[1,256,2,128]{3,1,0,2:T(8,128)(2,1)S(1)}, u32[]{:S(2)}, u32[]{:S(2)}) collective-permute-start(bf16[1,256,2,128]{3,1,0,2:T(8,128)(2,1)S(1)} %broadcast_select_fusion.8), channel_id=1, source_target_pairs={{0,16},{4,20},{8,24},{12,28},{16,0},{20,4},{24,8},{28,12},{1,17},{... | collective-permute-start | bytes 393224 | tf_op jit(solution)/shard_map/ppermute | solution.py:12
  37.6 16.2 %collective-permute-start.5 = (bf16[1,256,2,128]{3,1,0,2:T(8,128)(2,1)S(1)}, bf16[1,256,2,128]{3,1,0,2:T(8,128)(2,1)S(1)}, u32[]{:S(2)}, u32[]{:S(2)}) collective-permute-start(bf16[1,256,2,128]{3,1,0,2:T(8,128)(2,1)S(1)} %broadcast_select_fusion.5), channel_id=1, source_target_pairs={{0,16},{4,20},{8,24},{12,28},{16,0},{20,4},{24,8},{28,12},{1,17},{... | collective-permute-start | bytes 393224 | tf_op jit(solution)/shard_map/ppermute | solution.py:12
  40.4 19.8 %collective-permute-start.8 = (bf16[1,256,2,128]{3,1,0,2:T(8,128)(2,1)S(1)}, bf16[1,256,2,128]{3,1,0,2:T(8,128)(2,1)S(1)}, u32[]{:S(2)}, u32[]{:S(2)}) collective-permute-start(bf16[1,256,2,128]{3,1,0,2:T(8,128)(2,1)S(1)} %broadcast_select_fusion.2), channel_id=1, source_target_pairs={{0,16},{4,20},{8,24},{12,28},{16,0},{20,4},{24,8},{28,12},{1,17},{... | collective-permute-start | bytes 393224 | tf_op jit(solution)/shard_map/ppermute | solution.py:12
  77.2 5.8 %copy-start.1 = (bf16[1024,2048]{1,0:T(8,128)(2,1)S(1)}, bf16[1024,2048]{1,0:T(8,128)(2,1)}, u32[]{:S(2)}) copy-start(bf16[1024,2048]{1,0:T(8,128)(2,1)} %param.13) | copy-start | bytes 12582916
Sparse Core Ops, SparseCore 0:
  9.5 58.3 all-gather.1
  85.7 29.8 reduce-scatter.1
where the time goes:
time: 125 us; the launch traced here: 124 us
  waiting for transfers between devices  56.7 us (45%)
  starting transfers between devices  21.1 us (17%)
  between operations  19.4 us (16%)
  matrix products  15.3 us (12%)
  other arithmetic  5.95 us (5%)
  local copies, waits for them, and re-layouts  5.8 us (5%)
    reduce_scatter x1, waiting for transfers between devices, body(): lax.psum_scatter(group_terms, 'head', scatter_dimension=1, tiled=True)  30 us
    ppermute x9, starting transfers between devices, passed_along(): return lax.ppermute(value, axis, pairs)  21.1 us
    ppermute x9, waiting for transfers between devices, passed_along(): return lax.ppermute(value, axis, pairs)  18.5 us
    all_gather x1, waiting for transfers between devices, body(): whole_cache = lax.all_gather(cache_kv, 'seq', axis=0, tiled=True)  7.47 us
    sub x1, matrix products, body(): weights = jnp.exp(scores - row_max)  6.94 us
    dot_general x1, matrix products, body(): jnp.einsum('grk,kd->rgd', weights_bf, all_keys[:, 1, :], preferred_elemen...  5.73 us
    dot_general x1, matrix products, body(): jnp.dot(attended, out_proj, preferred_element_type=jnp.float32)  2.61 us
  transfers between devices with their start and end apart: 11, of which 8 were waited for; matrix products, arithmetic and copies ran while one was open for 6% of the time, Pallas kernels for 0%

commit v1 on v0

--- a/solution.py
+++ b/solution.py
@@ -4,6 +4,18 @@
 from jax.sharding import PartitionSpec as P
 
 PAGE = 128
+
+
+def collect(shard, axis, dim):
+    ways, here, turn = (lax.axis_size(axis), lax.axis_index(axis), shard.shape[dim])
+    line, have = (shard, 1)
+    while have < ways:
+        line = jnp.concatenate(
+            [line, lax.ppermute(line, axis, [(d, (d - have) % ways) for d in range(ways)])],
+            axis=dim,
+        )
+        have = 2 * have
+    return jnp.roll(line, here * turn, axis=dim)
 
 
 def passed_along(value, axis, steps):
@@ -43,7 +55,7 @@
     )
     per_shard = row_count // PAGE
     owners = page_ids // per_shard
-    whole_cache = lax.all_gather(cache_kv, "seq", axis=0, tiled=True)
+    whole_cache = collect(cache_kv, "seq", 0)
     vertical = jax.vmap(
         lambda page_key: lax.dynamic_slice_in_dim(whole_cache, page_key * PAGE, PAGE, 0)
     )(page_ids)

time: 125 us -> 143 us (1.14)
  waiting for transfers between devices: 56.7 us -> 78.9 us
  starting transfers between devices: 21.1 us -> 16.1 us
    ppermute x9, waiting for transfers between devices: 18.5 us -> 37.2 us  [passed_along(): return lax.ppermute(value, axis, pairs)]
    ppermute x9, starting transfers between devices: 21.1 us -> 3.66 us  [passed_along(): return lax.ppermute(value, axis, pairs)]
    ppermute x0 -> x3, starting transfers between devices: none -> 12.4 us  [collect(): lax.ppermute(line, axis, [(d, (d - have) % ways) for d in range(ways)])]
    ppermute x0 -> x3, waiting for transfers between devices: none -> 10.5 us  [collect(): lax.ppermute(line, axis, [(d, (d - have) % ways) for d in range(ways)])]
    all_gather x1 -> x0, waiting for transfers between devices: 7.47 us -> none  [body(): whole_cache = lax.all_gather(cache_kv, 'seq', axis=0, tiled=True)]
    unnamed x6 -> x17, local copies, waits for them, and re-layouts: 1.88 us -> 3.18 us
  transfers between devices with their start and end apart: 11 -> 13, of which waited for: 8 -> 10; matrix products, arithmetic and copies ran while one was open for 6% -> 6% of each run, Pallas kernels for 0% -> 0%
where the time goes in v1:
time: 143 us
  waiting for transfers between devices  78.9 us (55%)
  between operations  19.4 us (14%)
  starting transfers between devices  16.1 us (11%)
  matrix products  15.3 us (11%)
  other arithmetic  7.02 us (5%)
  local copies, waits for them, and re-layouts  6.3 us (4%)
    ppermute x9, waiting for transfers between devices, passed_along(): return lax.ppermute(value, axis, pairs)  37.2 us
    reduce_scatter x1, waiting for transfers between devices, body(): lax.psum_scatter(group_terms, 'head', scatter_dimension=1, tiled=True)  31.1 us
    ppermute x3, starting transfers between devices, collect(): lax.ppermute(line, axis, [(d, (d - have) % ways) for d in range(ways)])  12.4 us
    ppermute x3, waiting for transfers between devices, collect(): lax.ppermute(line, axis, [(d, (d - have) % ways) for d in range(ways)])  10.5 us
    sub x1, matrix products, body(): weights = jnp.exp(scores - row_max)  6.99 us
    dot_general x1, matrix products, body(): jnp.einsum('grk,kd->rgd', weights_bf, all_keys[:, 1, :], preferred_elemen...  5.75 us
    ppermute x9, starting transfers between devices, passed_along(): return lax.ppermute(value, axis, pairs)  3.66 us
    unnamed x17, local copies, waits for them, and re-layouts  3.18 us
  transfers between devices with their start and end apart: 13, of which 10 were waited for; matrix products, arithmetic and copies ran while one was open for 6% of the time, Pallas kernels for 0%

profile of v1, /device:TPU:0, one launch (start us, length us, event | category | flops | bytes accessed | tf_op | source)
XLA Modules:
  0.0 143.0 jit_solution(8583588583465561222)
XLA Ops:
  6.5 0.0 copy-start
  6.5 0.0 copy-start.1
  6.5 0.0 copy-start.2
  6.5 0.0 reduce-scatter.2.cloned.1.call-start
  6.5 6.1 %collective-permute-start.9 = (bf16[256,2,128]{2,1,0:T(2,128)(2,1)}, bf16[256,2,128]{2,1,0:T(2,128)(2,1)S(1)}, u32[]{:S(2)}, u32[]{:S(2)}) collective-permute-start(bf16[256,2,128]{2,1,0:T(2,128)(2,1)} %param.9), channel_id=1, source_target_pairs={{0,28},{4,0},{8,4},{12,8},{16,12},{20,16},{24,20},{28,24},{1,29},{... | collective-permute-start | bytes 393224 | tf_op jit(solution)/shard_map/ppermute | solution.py:14
  12.6 1.0 copy.16
  13.6 0.9 copy.18
  14.5 0.7 compare_bitcast_fusion
  15.2 0.1 broadcast_select_fusion
  15.3 0.1 collective-permute-start
  15.4 0.1 collective-permute-start.6
  15.5 0.5 collective-permute-start.3
  15.9 0.7 and_select_fusion
  16.6 0.7 fusion.23
  17.2 0.7 compare_bitcast_fusion.1
  17.9 0.7 subtract_bitcast_fusion
  18.6 0.1 broadcast_in_dim.154
  18.7 0.2 and_reduce_fusion
  18.9 0.1 broadcast_bitcast_fusion
  19.0 0.3 pad_add_fusion
  19.3 0.0 copy-done.2
  19.3 0.6 fusion.27
  25.7 0.0 copy-done.1
  25.7 0.1 constant_dynamic-update-slice_fusion.7
  25.8 0.0 collective-permute-done
  25.8 1.4 collective-permute-done.6
  27.2 1.4 collective-permute-done.3
  28.7 0.1 collective-permute-start.1
  28.8 0.0 collective-permute-done.9
  28.8 0.3 pad_maximum_fusion.3
  29.1 3.9 %collective-permute-start.10 = (bf16[512,2,128]{2,1,0:T(2,128)(2,1)S(1)}, bf16[512,2,128]{2,1,0:T(2,128)(2,1)S(1)}, u32[]{:S(2)}, u32[]{:S(2)}) collective-permute-start(bf16[512,2,128]{2,1,0:T(2,128)(2,1)S(1)} %pad_maximum_fusion.3), channel_id=1, source_target_pairs={{0,24},{4,28},{8,0},{12,4},{16,8},{20,12},{24,16},{28,20},{1,25},{... | collective-permute-start | bytes 786440 | tf_op jit(solution)/shard_map/ppermute | solution.py:14
  33.0 0.0 collective-permute-start.4
  33.0 0.0 collective-permute-start.7
  33.0 0.1 constant_dynamic-update-slice_fusion.6
  33.1 3.8 %collective-permute-done.1 = bf16[1,256,2,128]{3,1,0,2:T(8,128)(2,1)S(1)} collective-permute-done((bf16[1,256,2,128]{3,1,0,2:T(8,128)(2,1)S(1)}, bf16[1,256,2,128]{3,1,0,2:T(8,128)(2,1)S(1)}, u32[]{:S(2)}, u32[]{:S(2)}) %collective-permute-start.1) | collective-permute-done | bytes 131104 | tf_op jit(solution)/shard_map/ppermute | solution.py:24
  36.9 2.4 %collective-permute-start.2 = (bf16[1,256,2,128]{3,1,0,2:T(8,128)(2,1)S(1)}, bf16[1,256,2,128]{3,1,0,2:T(8,128)(2,1)S(1)}, u32[]{:S(2)}, u32[]{:S(2)}) collective-permute-start(bf16[1,256,2,128]{3,1,0,2:T(8,128)(2,1)S(1)} %broadcast_select_fusion.8), channel_id=1, source_target_pairs={{0,16},{4,20},{8,24},{12,28},{16,0},{20,4},{24,8},{28,12},{1,17},{... | collective-permute-start | bytes 393224 | tf_op jit(solution)/shard_map/ppermute | solution.py:24
  39.3 6.1 %collective-permute-done.4 = bf16[1,256,2,128]{3,1,0,2:T(8,128)(2,1)S(1)} collective-permute-done((bf16[1,256,2,128]{3,1,0,2:T(8,128)(2,1)S(1)}, bf16[1,256,2,128]{3,1,0,2:T(8,128)(2,1)S(1)}, u32[]{:S(2)}, u32[]{:S(2)}) %collective-permute-start.4) | collective-permute-done | bytes 131104 | tf_op jit(solution)/shard_map/ppermute | solution.py:24
  45.5 0.1 collective-permute-start.5
  45.5 2.7 %collective-permute-done.7 = bf16[1,256,2,128]{3,1,0,2:T(8,128)(2,1)S(1)} collective-permute-done((bf16[1,256,2,128]{3,1,0,2:T(8,128)(2,1)S(1)}, bf16[1,256,2,128]{3,1,0,2:T(8,128)(2,1)S(1)}, u32[]{:S(2)}, u32[]{:S(2)}) %collective-permute-start.7) | collective-permute-done | bytes 131104 | tf_op jit(solution)/shard_map/ppermute | solution.py:24
  48.3 0.5 collective-permute-start.8
  48.8 0.0 collective-permute-done.10
  48.8 0.7 pad_maximum_fusion.1
  49.5 2.5 %collective-permute-start.11 = (bf16[1024,2,128]{2,1,0:T(2,128)(2,1)S(1)}, bf16[1024,2,128]{2,1,0:T(2,128)(2,1)S(1)}, u32[]{:S(2)}, u32[]{:S(2)}) collective-permute-start(bf16[1024,2,128]{2,1,0:T(2,128)(2,1)S(1)} %pad_maximum_fusion.1), channel_id=1, source_target_pairs={{0,16},{4,20},{8,24},{12,28},{16,0},{20,4},{24,8},{28,12},{1,17},{... | collective-permute-start | bytes 1572872 | tf_op jit(solution)/shard_map/ppermute | solution.py:14
  52.0 16.4 %collective-permute-done.2 = bf16[1,256,2,128]{3,1,0,2:T(8,128)(2,1)S(1)} collective-permute-done((bf16[1,256,2,128]{3,1,0,2:T(8,128)(2,1)S(1)}, bf16[1,256,2,128]{3,1,0,2:T(8,128)(2,1)S(1)}, u32[]{:S(2)}, u32[]{:S(2)}) %collective-permute-start.2) | collective-permute-done | bytes 131104 | tf_op jit(solution)/shard_map/ppermute | solution.py:24
  68.5 2.8 %collective-permute-done.5 = bf16[1,256,2,128]{3,1,0,2:T(8,128)(2,1)S(1)} collective-permute-done((bf16[1,256,2,128]{3,1,0,2:T(8,128)(2,1)S(1)}, bf16[1,256,2,128]{3,1,0,2:T(8,128)(2,1)S(1)}, u32[]{:S(2)}, u32[]{:S(2)}) %collective-permute-start.5) | collective-permute-done | bytes 131104 | tf_op jit(solution)/shard_map/ppermute | solution.py:24
  71.3 0.2 constant_dynamic-update-slice_fusion.5
  71.5 2.6 %collective-permute-done.8 = bf16[1,256,2,128]{3,1,0,2:T(8,128)(2,1)S(1)} collective-permute-done((bf16[1,256,2,128]{3,1,0,2:T(8,128)(2,1)S(1)}, bf16[1,256,2,128]{3,1,0,2:T(8,128)(2,1)S(1)}, u32[]{:S(2)}, u32[]{:S(2)}) %collective-permute-start.8) | collective-permute-done | bytes 131104 | tf_op jit(solution)/shard_map/ppermute | solution.py:24
  74.1 10.5 %collective-permute-done.11 = bf16[1024,2,128]{2,1,0:T(2,128)(2,1)S(1)} collective-permute-done((bf16[1024,2,128]{2,1,0:T(2,128)(2,1)S(1)}, bf16[1024,2,128]{2,1,0:T(2,128)(2,1)S(1)}, u32[]{:S(2)}, u32[]{:S(2)}) %collective-permute-start.11) | collective-permute-done | bytes 524320 | tf_op jit(solution)/shard_map/ppermute | solution.py:14
  84.7 0.4 constant_dynamic-update-slice_fusion.4
  85.1 0.1 constant_dynamic-update-slice_fusion.3
  85.2 0.1 constant_dynamic-update-slice_fusion.2
  85.3 0.2 constant_dynamic-update-slice_fusion.1
  85.5 0.4 constant_dynamic-update-slice_fusion
  85.9 0.8 constant_dynamic-slice_fusion
  86.7 1.1 gather_fusion
  87.8 0.1 pad_maximum_fusion
  87.9 0.0 copy-done
  87.9 7.0 %fusion.28 = (f32[8,256]{1,0:T(8,128)S(1)}, f32[8,256,1536]{1,2,0:T(8,128)}) fusion(pred[256,1536]{0,1:T(8,128)(4,1)S(1)} %pad_add_fusion, bf16[1536,2,128]{2,0,1:T(8,128)(2,1)S(1)} %pad_maximum_fusion, bf16[256,1024]{1,0:T(8,128)(2,1)S(1)} %copy-done), kind=kOutput, calls=%fused_computation.65 | convolution fusion | flops 817890816 | bytes 13901824 | tf_op jit(solution)/shard_map/sub | solution.py:86
  94.9 5.7 %fusion.8 = bf16[128,8,256]{2,0,1:T(8,128)(2,1)S(1)} fusion(f32[8,256,1536]{1,2,0:T(8,128)} %get-tuple-element.17, f32[8,256]{1,0:T(8,128)S(1)} %get-tuple-element.16, bf16[1536,2,128]{2,0,1:T(8,128)(2,1)S(1)} %pad_maximum_fusion), kind=kOutput, calls=%fused_computation.12 | convolution fusion | flops 811859968 | bytes 13508608 | tf_op jit(solution)/shard_map/grk,kd->rgd/dot_general | solution.py:89
  100.7 0.0 copy-done.3
  100.7 2.6 %fusion.33 = f32[256,2048]{1,0:T(8,128)} fusion(bf16[256,1024]{0,1:T(8,128)(2,1)S(1)} %bitcast.95, bf16[1024,2048]{1,0:T(8,128)(2,1)S(1)} %copy-done.3), kind=kOutput, calls=%fused_computation.66 | convolution fusion | flops 1073741824 | bytes 6815744 | tf_op jit(solution)/shard_map/dot_general | solution.py:93
  103.3 0.0 reduce-scatter.2.cloned.1.call-update
  103.3 31.1 %reduce-scatter.2.cloned.1.call-done = f32[256,512]{1,0:T(8,128)} async-done(((f32[256,2048]{1,0:T(8,128)}), f32[256,512]{1,0:T(8,128)}) %reduce-scatter.2.cloned.1.call-update) | async-done | bytes 524304 | tf_op jit(solution)/shard_map/reduce_scatter | solution.py:94
  134.4 1.8 %convert_element_type.15 = bf16[256,512]{1,0:T(8,128)(2,1)} convert(f32[256,512]{1,0:T(8,128)} %reduce-scatter.2.cloned.1.call-done) | non-fusion elementwise | flops 131072 | bytes 786432 | tf_op jit(solution)/shard_map/convert_element_type | solution.py:94
  (16 shorter events, 0.3 us)
Async XLA Ops:
  6.5 81.4 %copy-start = (bf16[256,1024]{1,0:T(8,128)(2,1)S(1)}, bf16[256,1024]{1,0:T(8,128)(2,1)}, u32[]{:S(2)}) copy-start(bf16[256,1024]{1,0:T(8,128)(2,1)} %param.7) | copy-start | bytes 1572868
  6.5 19.2 %copy-start.1 = (bf16[256,2,128]{2,1,0:T(2,128)(2,1)S(1)}, bf16[256,2,128]{2,1,0:T(2,128)(2,1)}, u32[]{:S(2)}) copy-start(bf16[256,2,128]{2,1,0:T(2,128)(2,1)} %param.9) | copy-start | bytes 393220
  6.5 12.7 %copy-start.2 = (s32[1,3]{1,0:T(1,128)S(1)}, s32[1,3]{1,0:T(1,128)}, u32[]{:S(2)}) copy-start(s32[1,3]{1,0:T(1,128)} %param.11) | copy-start | bytes 40
  6.5 127.9 %reduce-scatter.2.cloned.1.call-start = ((), (), s32[]{:S(2)}) async-start(), calls=%async_computation.1 | async-start | bytes 2621440 | tf_op jit(solution)/shard_map/reduce_scatter | solution.py:94
  6.5 22.2 %collective-permute-start.9 = (bf16[256,2,128]{2,1,0:T(2,128)(2,1)}, bf16[256,2,128]{2,1,0:T(2,128)(2,1)S(1)}, u32[]{:S(2)}, u32[]{:S(2)}) collective-permute-start(bf16[256,2,128]{2,1,0:T(2,128)(2,1)} %param.9), channel_id=1, source_target_pairs={{0,28},{4,0},{8,4},{12,8},{16,12},{20,16},{24,20},{28,24},{1,29},{... | collective-permute-start | bytes 393224 | tf_op jit(solution)/shard_map/ppermute | solution.py:14
  15.3 10.5 %collective-permute-start = (bf16[1,256,2,128]{3,1,0,2:T(8,128)(2,1)S(1)}, bf16[1,256,2,128]{3,1,0,2:T(8,128)(2,1)S(1)}, u32[]{:S(2)}, u32[]{:S(2)}) collective-permute-start(bf16[1,256,2,128]{3,1,0,2:T(8,128)(2,1)S(1)} %get-tuple-element.8), channel_id=1, source_target_pairs={{0,4},{4,8},{8,12},{12,16},{16,20},{20,24},{24,28},{28,0},{1,5},{5... | collective-permute-start | bytes 393224 | tf_op jit(solution)/shard_map/ppermute | solution.py:24
  15.4 11.9 %collective-permute-start.6 = (bf16[1,256,2,128]{3,1,0,2:T(8,128)(2,1)S(1)}, bf16[1,256,2,128]{3,1,0,2:T(8,128)(2,1)S(1)}, u32[]{:S(2)}, u32[]{:S(2)}) collective-permute-start(bf16[1,256,2,128]{3,1,0,2:T(8,128)(2,1)S(1)} %get-tuple-element.9), channel_id=1, source_target_pairs={{0,4},{4,8},{8,12},{12,16},{16,20},{20,24},{24,28},{28,0},{1,5},{5... | collective-permute-start | bytes 393224 | tf_op jit(solution)/shard_map/ppermute | solution.py:24
  15.5 13.2 %collective-permute-start.3 = (bf16[1,256,2,128]{3,1,0,2:T(8,128)(2,1)S(1)}, bf16[1,256,2,128]{3,1,0,2:T(8,128)(2,1)S(1)}, u32[]{:S(2)}, u32[]{:S(2)}) collective-permute-start(bf16[1,256,2,128]{3,1,0,2:T(8,128)(2,1)S(1)} %get-tuple-element.10), channel_id=1, source_target_pairs={{0,4},{4,8},{8,12},{12,16},{16,20},{20,24},{24,28},{28,0},{1,5},{5... | collective-permute-start | bytes 393224 | tf_op jit(solution)/shard_map/ppermute | solution.py:24
  28.7 8.2 %collective-permute-start.1 = (bf16[1,256,2,128]{3,1,0,2:T(8,128)(2,1)S(1)}, bf16[1,256,2,128]{3,1,0,2:T(8,128)(2,1)S(1)}, u32[]{:S(2)}, u32[]{:S(2)}) collective-permute-start(bf16[1,256,2,128]{3,1,0,2:T(8,128)(2,1)S(1)} %get-tuple-element.5), channel_id=1, source_target_pairs={{0,8},{4,12},{8,16},{12,20},{16,24},{20,28},{24,0},{28,4},{1,9},{5... | collective-permute-start | bytes 393224 | tf_op jit(solution)/shard_map/ppermute | solution.py:24
  29.1 19.7 %collective-permute-start.10 = (bf16[512,2,128]{2,1,0:T(2,128)(2,1)S(1)}, bf16[512,2,128]{2,1,0:T(2,128)(2,1)S(1)}, u32[]{:S(2)}, u32[]{:S(2)}) collective-permute-start(bf16[512,2,128]{2,1,0:T(2,128)(2,1)S(1)} %pad_maximum_fusion.3), channel_id=1, source_target_pairs={{0,24},{4,28},{8,0},{12,4},{16,8},{20,12},{24,16},{28,20},{1,25},{... | collective-permute-start | bytes 786440 | tf_op jit(solution)/shard_map/ppermute | solution.py:14
  33.0 12.5 %collective-permute-start.4 = (bf16[1,256,2,128]{3,1,0,2:T(8,128)(2,1)S(1)}, bf16[1,256,2,128]{3,1,0,2:T(8,128)(2,1)S(1)}, u32[]{:S(2)}, u32[]{:S(2)}) collective-permute-start(bf16[1,256,2,128]{3,1,0,2:T(8,128)(2,1)S(1)} %get-tuple-element.6), channel_id=1, source_target_pairs={{0,8},{4,12},{8,16},{12,20},{16,24},{20,28},{24,0},{28,4},{1,9},{5... | collective-permute-start | bytes 393224 | tf_op jit(solution)/shard_map/ppermute | solution.py:24
  33.0 15.3 %collective-permute-start.7 = (bf16[1,256,2,128]{3,1,0,2:T(8,128)(2,1)S(1)}, bf16[1,256,2,128]{3,1,0,2:T(8,128)(2,1)S(1)}, u32[]{:S(2)}, u32[]{:S(2)}) collective-permute-start(bf16[1,256,2,128]{3,1,0,2:T(8,128)(2,1)S(1)} %get-tuple-element.7), channel_id=1, source_target_pairs={{0,8},{4,12},{8,16},{12,20},{16,24},{20,28},{24,0},{28,4},{1,9},{5... | collective-permute-start | bytes 393224 | tf_op jit(solution)/shard_map/ppermute | solution.py:24
  36.9 31.5 %collective-permute-start.2 = (bf16[1,256,2,128]{3,1,0,2:T(8,128)(2,1)S(1)}, bf16[1,256,2,128]{3,1,0,2:T(8,128)(2,1)S(1)}, u32[]{:S(2)}, u32[]{:S(2)}) collective-permute-start(bf16[1,256,2,128]{3,1,0,2:T(8,128)(2,1)S(1)} %broadcast_select_fusion.8), channel_id=1, source_target_pairs={{0,16},{4,20},{8,24},{12,28},{16,0},{20,4},{24,8},{28,12},{1,17},{... | collective-permute-start | bytes 393224 | tf_op jit(solution)/shard_map/ppermute | solution.py:24
  45.5 25.8 %collective-permute-start.5 = (bf16[1,256,2,128]{3,1,0,2:T(8,128)(2,1)S(1)}, bf16[1,256,2,128]{3,1,0,2:T(8,128)(2,1)S(1)}, u32[]{:S(2)}, u32[]{:S(2)}) collective-permute-start(bf16[1,256,2,128]{3,1,0,2:T(8,128)(2,1)S(1)} %broadcast_select_fusion.5), channel_id=1, source_target_pairs={{0,16},{4,20},{8,24},{12,28},{16,0},{20,4},{24,8},{28,12},{1,17},{... | collective-permute-start | bytes 393224 | tf_op jit(solution)/shard_map/ppermute | solution.py:24
  48.3 25.8 %collective-permute-start.8 = (bf16[1,256,2,128]{3,1,0,2:T(8,128)(2,1)S(1)}, bf16[1,256,2,128]{3,1,0,2:T(8,128)(2,1)S(1)}, u32[]{:S(2)}, u32[]{:S(2)}) collective-permute-start(bf16[1,256,2,128]{3,1,0,2:T(8,128)(2,1)S(1)} %broadcast_select_fusion.2), channel_id=1, source_target_pairs={{0,16},{4,20},{8,24},{12,28},{16,0},{20,4},{24,8},{28,12},{1,17},{... | collective-permute-start | bytes 393224 | tf_op jit(solution)/shard_map/ppermute | solution.py:24
  49.5 35.1 %collective-permute-start.11 = (bf16[1024,2,128]{2,1,0:T(2,128)(2,1)S(1)}, bf16[1024,2,128]{2,1,0:T(2,128)(2,1)S(1)}, u32[]{:S(2)}, u32[]{:S(2)}) collective-permute-start(bf16[1024,2,128]{2,1,0:T(2,128)(2,1)S(1)} %pad_maximum_fusion.1), channel_id=1, source_target_pairs={{0,16},{4,20},{8,24},{12,28},{16,0},{20,4},{24,8},{28,12},{1,17},{... | collective-permute-start | bytes 1572872 | tf_op jit(solution)/shard_map/ppermute | solution.py:14
  94.9 5.8 %copy-start.3 = (bf16[1024,2048]{1,0:T(8,128)(2,1)S(1)}, bf16[1024,2048]{1,0:T(8,128)(2,1)}, u32[]{:S(2)}) copy-start(bf16[1024,2048]{1,0:T(8,128)(2,1)} %param.13) | copy-start | bytes 12582916
Sparse Core Ops, SparseCore 0:
  103.4 30.9 reduce-scatter.1
